TPU v7x, 256 devices: a whole 4x4x8 slice. The times are simulated.
256 devices in a mesh: aux: 2 (over core), row: 8 (over z), col: 16 (over x, y).
Axes of the slice: x: 4, y: 4, z: 8, core: 2. Of those that a mesh axis runs over, the one named last changes fastest.
Arguments:
- coulomb: bfloat16 [64, 2048, 2048], P('aux', 'row', 'col'), may hold values from -6 to 6
- occupied: bfloat16 [2048, 2048], P('row'), may hold values from -0.125 to 0.125
- virtual: bfloat16 [2048, 2048], P('row'), may hold values from -0.125 to 0.125
- tile_mask: int32 [16, 16], replicated, may hold values 0 or 1
Outputs:
- chi: float32 [64, 64], P('aux')
All inputs are finite; a program needn't handle non-finite values.
Results may differ from a plain program's by a relative error of at most 0.0042.
Values may be sent and summed in bfloat16 or wider, within the bound.
A program may use at most 128 MiB of HBM per device.

v0:
```python
import jax
import jax.numpy as jnp
from jax import lax
from jax.sharding import PartitionSpec as P

NAO = 2048
TILE = 128


def swapped(value, axis, apart):
    mask = 2**apart
    pairs = [(source, source ^ mask) for source in range(lax.axis_size(axis))]
    return lax.ppermute(value, axis, pairs)


def shards(coulomb, occupied, virtual, tile_mask):
    rows = lax.axis_size("row")
    cols = lax.axis_size("col")
    pdev, mrow, ncol = coulomb.shape
    nao = mrow * rows
    row_idx = lax.axis_index("row")
    col_idx = lax.axis_index("col")
    aux_idx = lax.axis_index("aux")
    tiles_r = mrow // TILE
    tiles_c = ncol // TILE
    local_tiles = lax.dynamic_slice(
        tile_mask, (row_idx * tiles_r, col_idx * tiles_c), (tiles_r, tiles_c)
    )
    local_mask = jnp.repeat(jnp.repeat(local_tiles, TILE, axis=0), TILE, axis=1).astype(
        jnp.bfloat16
    )
    screened = coulomb * local_mask[None]
    moved = lax.all_to_all(screened, "row", split_axis=0, concat_axis=1, tiled=True)
    pieces = moved.shape[0]
    occ_all, virt_all = (
        lax.all_gather(occupied, "row", axis=0, tiled=True),
        lax.all_gather(virtual, "row", axis=0, tiled=True),
    )
    half = jnp.einsum("ml,pmn->pln", occ_all, moved, preferred_element_type=jnp.float32).astype(
        jnp.bfloat16
    )
    jpart = mrow // cols
    shaped = half.reshape(pieces, rows, cols, jpart, ncol)
    spread = lax.all_to_all(shaped, "col", split_axis=2, concat_axis=4, tiled=True)
    spread = spread.reshape(pieces, rows * jpart, nao)
    dressed = jnp.einsum(
        "pln,ns->pls", spread, virt_all, preferred_element_type=jnp.float32
    ).astype(jnp.bfloat16)
    layered = dressed.reshape(pieces, rows, 1, jpart, cols, ncol)
    returned = lax.all_to_all(
        lax.all_to_all(layered, "row", split_axis=1, concat_axis=0, tiled=True),
        "col",
        split_axis=4,
        concat_axis=2,
        tiled=True,
    )
    aligned = returned.reshape(pdev, mrow, ncol)
    theirs = swapped(screened, "aux", 0)
    with_mine = jnp.einsum("pls,qls->pq", aligned, screened, preferred_element_type=jnp.float32)
    with_theirs = jnp.einsum("pls,qls->pq", aligned, theirs, preferred_element_type=jnp.float32)
    first_half = jnp.where(aux_idx == 0, with_mine, with_theirs)
    second_half = jnp.where(aux_idx == 0, with_theirs, with_mine)
    partial_chi = jnp.concatenate([first_half, second_half], axis=1)
    slots = lax.axis_size("aux")
    placed = jnp.zeros((slots,) + partial_chi.shape, partial_chi.dtype)
    placed = lax.dynamic_update_index_in_dim(placed, partial_chi, aux_idx, 0)
    total = lax.psum(placed, ("aux", "row", "col"))
    total_chi = lax.dynamic_index_in_dim(total, aux_idx, 0, keepdims=False)
    return total_chi / NAO


def solution(mesh):
    placed = (P("aux", "row", "col"), P("row", None), P("row", None), P())
    return jax.shard_map(
        shards, mesh=mesh, in_specs=placed, out_specs=P("aux", None), check_vma=False
    )
```

profile of v0, /device:TPU:1, one launch (start us, length us, event | category | flops | bytes accessed | tf_op | source)
XLA Modules:
  0.0 430.4 jit_solution(17136864265026919637)
XLA Ops:
  6.5 0.0 all-gather.3.cloned.1.call-start
  6.5 0.7 all-gather.3.cloned.1.call-update
  7.3 0.0 all-gather.5.cloned.1.call-start
  7.3 0.7 all-gather.5.cloned.1.call-update
  8.0 0.9 fusion.14
  8.9 0.1 broadcast_bitcast_fusion
  9.0 2.8 copy_multiply_fusion
  11.7 0.8 copy.15
  12.6 79.7 %all_to_all.66 = bf16[32,256,128]{2,1,0:T(8,128)(2,1)} all-to-all(bf16[32,256,128]{2,1,0:T(8,128)(2,1)S(1)} %copy.15), channel_id=1, replica_groups=mesh['aux'=2,'row'=8,'col'=16] {'row'}, dimensions={0} | all-to-all | bytes 4194304 | tf_op jit(solution)/shard_map/all_to_all | solution.py:33
  92.2 4.5 %copy.16 = bf16[8,4,256,128]{2,0,3,1:T(8,128)(2,1)} copy(bf16[8,4,256,128]{3,2,1,0:T(8,128)(2,1)} %bitcast.62) | data formatting | bytes 4194304 | tf_op jit(solution)/shard_map/all_to_all | solution.py:33
  96.7 4.2 all_to_all.51
  100.9 48.7 %all-gather.3.cloned.1.call-done = bf16[2048,2048]{1,0:T(8,128)(2,1)} async-done(((bf16[256,2048]{1,0:T(8,128)(2,1)}), bf16[2048,2048]{1,0:T(8,128)(2,1)}) %all-gather.3.cloned.1.call-update) | async-done | bytes 8388624 | tf_op jit(solution)/shard_map/all_gather | solution.py:36
  149.7 9.8 %fusion.10 = bf16[4,2048,128]{1,2,0:T(8,128)(2,1)} fusion(bf16[4,2048,128]{1,2,0:T(8,128)(2,1)} %all_to_all.51, bf16[2048,2048]{1,0:T(8,128)(2,1)} %all-gather.3.cloned.1.call-done), kind=kOutput, calls=%fused_computation.6 | convolution fusion | flops 4296015872 | bytes 12582912 | tf_op jit(solution)/shard_map/ml,pmn->pln/dot_general | solution.py:39
  159.5 4.0 copy.17
  163.4 2.2 copy.18
  165.6 33.7 %all_to_all.67 = bf16[4,8,16,16,128]{4,3,1,0,2:T(8,128)(2,1)S(1)} all-to-all(bf16[4,8,16,16,128]{4,3,1,0,2:T(8,128)(2,1)S(1)} %copy.18), channel_id=1, replica_groups=mesh['aux'=2,'row'=8,'col'=16] {'col'}, dimensions={2} | all-to-all | bytes 4194304 | tf_op jit(solution)/shard_map/all_to_all | solution.py:44
  199.3 3.7 copy.19
  203.1 4.2 reshape.37
  207.3 37.2 %all-gather.5.cloned.1.call-done = bf16[2048,2048]{1,0:T(8,128)(2,1)} async-done(((bf16[256,2048]{1,0:T(8,128)(2,1)}), bf16[2048,2048]{1,0:T(8,128)(2,1)}) %all-gather.5.cloned.1.call-update) | async-done | bytes 8388624 | tf_op jit(solution)/shard_map/all_gather | solution.py:37
  244.4 8.5 %fusion.7 = bf16[4,128,2048]{2,1,0:T(8,128)(2,1)S(1)} fusion(bf16[4,128,2048]{2,1,0:T(8,128)(2,1)} %reshape.37, bf16[2048,2048]{1,0:T(8,128)(2,1)} %all-gather.5.cloned.1.call-done), kind=kOutput, calls=%fused_computation.5 | convolution fusion | flops 4296015872 | bytes 12582912 | tf_op jit(solution)/shard_map/pln,ns->pls/dot_general | solution.py:46
  253.0 0.6 copy.23
  253.6 0.6 copy.20
  254.2 53.5 %all_to_all.68 = bf16[4,8,1,16,16,128]{5,4,3,0,2,1:T(8,128)(2,1)S(1)} all-to-all(bf16[4,8,1,16,16,128]{5,4,3,0,2,1:T(8,128)(2,1)S(1)} %copy.20), channel_id=1, replica_groups=mesh['aux'=2,'row'=8,'col'=16] {'row'}, dimensions={1} | all-to-all | bytes 4194304 | tf_op jit(solution)/shard_map/all_to_all | solution.py:51
  307.7 1.8 copy.21
  309.6 6.6 %all-to-all-start.3 = ((bf16[32,1,1,16,16,128]{5,3,0,2,1,4:T(8,128)(2,1)}), bf16[32,1,1,16,16,128]{5,3,0,2,1,4:T(8,128)(2,1)}, u32[]{:S(2)}, u32[]{:S(2)}) async-start(bf16[32,1,1,16,16,128]{5,3,0,2,1,4:T(8,128)(2,1)} %copy.21), calls=%async_computation.3 | async-start | bytes 4194304 | tf_op jit(solution)/shard_map/all_to_all | solution.py:50
  316.2 2.8 collective-permute-start
  319.0 22.5 %all-to-all-done.3 = bf16[32,1,1,16,16,128]{5,3,0,2,1,4:T(8,128)(2,1)} async-done(((bf16[32,1,1,16,16,128]{5,3,0,2,1,4:T(8,128)(2,1)}), bf16[32,1,1,16,16,128]{5,3,0,2,1,4:T(8,128)(2,1)}, u32[]{:S(2)}, u32[]{:S(2)}) %all-to-all-start.3) | async-done | bytes 2097184 | tf_op jit(solution)/shard_map/all_to_all | solution.py:50
  341.5 2.1 copy.22
  343.6 0.7 convolution_bitcast_fusion.1
  344.3 0.0 collective-permute-done
  344.3 2.3 broadcast_select_fusion.1
  346.6 0.1 fusion.13
  346.7 76.2 %psum.7 = f32[2,32,64]{2,1,0:T(8,128)S(1)} all-reduce(f32[2,32,64]{2,1,0:T(8,128)S(1)} %fusion.13), channel_id=1, replica_groups=mesh['aux'=2,'row'=8,'col'=16] {'aux','row','col'}, use_global_device_ids=true, to_apply=%region_0.1 | all-reduce | flops 4096 | bytes 32768 | tf_op jit(solution)/shard_map/psum | solution.py:67
  422.9 0.6 multiply_bitcast_fusion
  (1 shorter events, 0.0 us)
Async XLA Ops:
  6.5 143.1 %all-gather.3.cloned.1.call-start = ((), (), s32[]{:S(2)}) async-start(), calls=%async_computation.4 | async-start | bytes 9437184 | tf_op jit(solution)/shard_map/all_gather | solution.py:36
  7.3 237.2 %all-gather.5.cloned.1.call-start = ((), (), s32[]{:S(2)}) async-start(), calls=%async_computation.5 | async-start | bytes 9437184 | tf_op jit(solution)/shard_map/all_gather | solution.py:37
  309.6 31.9 %all-to-all-start.3 = ((bf16[32,1,1,16,16,128]{5,3,0,2,1,4:T(8,128)(2,1)}), bf16[32,1,1,16,16,128]{5,3,0,2,1,4:T(8,128)(2,1)}, u32[]{:S(2)}, u32[]{:S(2)}) async-start(bf16[32,1,1,16,16,128]{5,3,0,2,1,4:T(8,128)(2,1)} %copy.21), calls=%async_computation.3 | async-start | bytes 4194304 | tf_op jit(solution)/shard_map/all_to_all | solution.py:50
  316.2 28.2 %collective-permute-start = (bf16[32,256,128]{2,0,1:T(8,128)(2,1)S(1)}, bf16[32,256,128]{2,0,1:T(8,128)(2,1)}, u32[]{:S(2)}, u32[]{:S(2)}) collective-permute-start(bf16[32,256,128]{2,0,1:T(8,128)(2,1)S(1)} %copy_multiply_fusion), channel_id=1, source_target_pairs={{0,128},{128,0},{1,129},{129,1},{2,130},{130,2},{3,131},{131,3},{4... | collective-permute-start | bytes 6291464 | tf_op jit(solution)/shard_map/ppermute | solution.py:13
Sparse Core Ops, SparseCore 0:
  9.1 140.4 all-gather.2
  151.4 92.9 all-gather.4
where the time goes:
time: 431 us; the launch traced here: 430 us
  blocking collectives  243 us (56%)
  waiting for transfers between devices  110 us (26%)
  local copies, waits for them, and re-layouts  28.9 us (7%)
  matrix products  21.3 us (5%)
  between operations  13.5 us (3%)
  starting transfers between devices  9.44 us (2%)
  other arithmetic  4.33 us (1%)
    all_to_all x1, blocking collectives, shards(): lax.all_to_all(screened, 'row', split_axis=0, concat_axis=1, tiled=True)  79.7 us
    psum x1, blocking collectives, shards(): total = lax.psum(placed, ('aux', 'row', 'col'))  76.2 us
    all_to_all x1, blocking collectives, shards(): lax.all_to_all(layered, 'row', split_axis=1, concat_axis=0, tiled=True)  53.5 us
    all_gather x1, waiting for transfers between devices, shards(): lax.all_gather(occupied, 'row', axis=0, tiled=True)  48.7 us
    all_gather x1, waiting for transfers between devices, shards(): lax.all_gather(virtual, 'row', axis=0, tiled=True)  37.2 us
    all_to_all x1, blocking collectives, shards(): lax.all_to_all(shaped, 'col', split_axis=2, concat_axis=4, tiled=True)  33.7 us
    all_to_all x1, waiting for transfers between devices, shards(): lax.all_to_all(lax.all_to_all(layered, 'row', split_axis=1, concat_axis=0...  22.5 us
    dot_general x1, matrix products, shards(): jnp.einsum('ml,pmn->pln', occ_all, moved, preferred_element_type=jnp.floa...  9.81 us
  transfers between devices with their start and end apart: 4, of which 3 were waited for; matrix products, arithmetic and copies ran while one was open for 8% of the time, Pallas kernels for 0%

commit v1 on v0

--- a/solution.py
+++ b/solution.py
@@ -5,6 +5,16 @@
 
 NAO = 2048
 TILE = 128
+
+
+def _process_table(array_in):
+    kept_arr = jnp.concatenate(
+        jax.lax.all_to_all(
+            jnp.stack(tuple((array_in for _ in range(jax.lax.psum(1, "row"))))), "row", 0, 0
+        ),
+        0,
+    )
+    return kept_arr
 
 
 def swapped(value, axis, apart):
@@ -33,7 +43,7 @@
     moved = lax.all_to_all(screened, "row", split_axis=0, concat_axis=1, tiled=True)
     pieces = moved.shape[0]
     occ_all, virt_all = (
-        lax.all_gather(occupied, "row", axis=0, tiled=True),
+        _process_table(occupied),
         lax.all_gather(virtual, "row", axis=0, tiled=True),
     )
     half = jnp.einsum("ml,pmn->pln", occ_all, moved, preferred_element_type=jnp.float32).astype(

time: 431 us -> 585 us (1.36)
  waiting for transfers between devices: 110 us -> 282 us
  blocking collectives: 243 us -> 221 us
    all_to_all x0 -> x1, waiting for transfers between devices: none -> 261 us  [_process_table(): jax.lax.all_to_all(jnp.stack(tuple((array_in for _ in range(jax.lax.psum(...]
    all_gather x1 -> x0, waiting for transfers between devices: 48.7 us -> none  [shards(): lax.all_gather(occupied, 'row', axis=0, tiled=True)]
    all_gather x1, waiting for transfers between devices: 37.2 us -> 0.01 us  [shards(): lax.all_gather(virtual, 'row', axis=0, tiled=True)]
    all_to_all x1, blocking collectives: 79.7 us -> 58.7 us  [shards(): lax.all_to_all(screened, 'row', split_axis=0, concat_axis=1, tiled=True)]
  transfers between devices with their start and end apart: 4 -> 4, of which waited for: 3 -> 2; matrix products, arithmetic and copies ran while one was open for 8% -> 5% of each run, Pallas kernels for 0% -> 0%
where the time goes in v1:
time: 585 us; the launch traced here: 584 us
  waiting for transfers between devices  282 us (48%)
  blocking collectives  221 us (38%)
  local copies, waits for them, and re-layouts  28.3 us (5%)
  matrix products  21.3 us (4%)
  starting transfers between devices  13.5 us (2%)
  between operations  13.5 us (2%)
    all_to_all x1, waiting for transfers between devices, _process_table(): jax.lax.all_to_all(jnp.stack(tuple((array_in for _ in range(jax.lax.psum(...  261 us
    psum x1, blocking collectives, shards(): total = lax.psum(placed, ('aux', 'row', 'col'))  77.7 us
    all_to_all x1, blocking collectives, shards(): lax.all_to_all(screened, 'row', split_axis=0, concat_axis=1, tiled=True)  58.7 us
    all_to_all x1, blocking collectives, shards(): lax.all_to_all(layered, 'row', split_axis=1, concat_axis=0, tiled=True)  50.7 us
    all_to_all x1, blocking collectives, shards(): lax.all_to_all(shaped, 'col', split_axis=2, concat_axis=4, tiled=True)  33.7 us
    all_to_all x1, waiting for transfers between devices, shards(): lax.all_to_all(lax.all_to_all(layered, 'row', split_axis=1, concat_axis=0...  21.2 us
  transfers between devices with their start and end apart: 4, of which 2 were waited for; matrix products, arithmetic and copies ran while one was open for 5% of the time, Pallas kernels for 0%

profile of v1, /device:TPU:1, one launch (start us, length us, event | category | flops | bytes accessed | tf_op | source)
XLA Modules:
  0.0 584.2 jit_solution(5476880884890782233)
XLA Ops:
  6.5 0.9 fusion.14
  7.4 0.1 broadcast_bitcast_fusion
  7.5 2.8 copy_multiply_fusion
  10.3 0.8 copy.15
  11.1 0.0 copy-start
  11.1 58.7 %all_to_all.68 = bf16[32,256,128]{2,1,0:T(8,128)(2,1)} all-to-all(bf16[32,256,128]{2,1,0:T(8,128)(2,1)S(1)} %copy.15), channel_id=1, replica_groups=mesh['aux'=2,'row'=8,'col'=16] {'row'}, dimensions={0} | all-to-all | bytes 4194304 | tf_op jit(solution)/shard_map/all_to_all | solution.py:43
  69.8 0.0 copy-done
  69.8 4.3 stack.2
  74.1 5.0 all-to-all-start.1
  79.1 0.0 all-gather.2.cloned.1.call-start
  79.2 0.7 all-gather.2.cloned.1.call-update
  79.9 3.9 copy.16
  83.8 260.5 %all-to-all-done.1 = bf16[8,256,2048]{2,1,0:T(8,128)(2,1)} async-done(((bf16[8,256,2048]{2,1,0:T(8,128)(2,1)}), bf16[8,256,2048]{2,1,0:T(8,128)(2,1)}, u32[]{:S(2)}, u32[]{:S(2)}) %all-to-all-start.1) | async-done | bytes 8388640 | tf_op jit(solution)/shard_map/all_to_all | solution.py:12
  344.3 9.8 %fusion.9 = bf16[4,2048,128]{1,2,0:T(8,128)(2,1)} fusion(bf16[8,256,2048]{2,1,0:T(8,128)(2,1)} %all-to-all-done.1, bf16[8,4,256,128]{2,3,1,0:T(8,128)(2,1)} %copy.16), kind=kOutput, calls=%fused_computation.6 | convolution fusion | flops 4296015872 | bytes 12582912 | tf_op jit(solution)/shard_map/ml,pmn->pln/dot_general | solution.py:49
  354.1 3.9 copy.17
  358.1 2.2 copy.18
  360.3 33.7 %all_to_all.69 = bf16[4,8,16,16,128]{4,3,1,0,2:T(8,128)(2,1)S(1)} all-to-all(bf16[4,8,16,16,128]{4,3,1,0,2:T(8,128)(2,1)S(1)} %copy.18), channel_id=1, replica_groups=mesh['aux'=2,'row'=8,'col'=16] {'col'}, dimensions={2} | all-to-all | bytes 4194304 | tf_op jit(solution)/shard_map/all_to_all | solution.py:54
  394.0 3.7 copy.19
  397.7 4.2 reshape.40
  401.9 0.0 all-gather.2.cloned.1.call-done
  401.9 8.5 %fusion.6 = bf16[4,128,2048]{2,1,0:T(8,128)(2,1)S(1)} fusion(bf16[4,128,2048]{2,1,0:T(8,128)(2,1)} %reshape.40, bf16[2048,2048]{1,0:T(8,128)(2,1)} %all-gather.2.cloned.1.call-done), kind=kOutput, calls=%fused_computation.5 | convolution fusion | flops 4296015872 | bytes 12582912 | tf_op jit(solution)/shard_map/pln,ns->pls/dot_general | solution.py:56
  410.5 0.6 copy.24
  411.1 0.6 copy.20
  411.7 50.7 %all_to_all.70 = bf16[4,8,1,16,16,128]{5,4,3,0,2,1:T(8,128)(2,1)S(1)} all-to-all(bf16[4,8,1,16,16,128]{5,4,3,0,2,1:T(8,128)(2,1)S(1)} %copy.20), channel_id=1, replica_groups=mesh['aux'=2,'row'=8,'col'=16] {'row'}, dimensions={1} | all-to-all | bytes 4194304 | tf_op jit(solution)/shard_map/all_to_all | solution.py:61
  462.4 1.8 copy.21
  464.2 4.5 all-to-all-start.4
  468.8 3.9 collective-permute-start
  472.7 21.2 %all-to-all-done.4 = bf16[32,1,1,16,16,128]{5,3,0,2,1,4:T(8,128)(2,1)} async-done(((bf16[32,1,1,16,16,128]{5,3,0,2,1,4:T(8,128)(2,1)}), bf16[32,1,1,16,16,128]{5,3,0,2,1,4:T(8,128)(2,1)}, u32[]{:S(2)}, u32[]{:S(2)}) %all-to-all-start.4) | async-done | bytes 2097184 | tf_op jit(solution)/shard_map/all_to_all | solution.py:60
  493.8 2.1 copy.22
  496.0 0.7 convolution_bitcast_fusion.1
  496.7 0.0 collective-permute-done
  496.7 2.3 broadcast_select_fusion.1
  499.0 0.1 fusion.13
  499.1 77.7 %psum.7 = f32[2,32,64]{2,1,0:T(8,128)S(1)} all-reduce(f32[2,32,64]{2,1,0:T(8,128)S(1)} %fusion.13), channel_id=1, replica_groups=mesh['aux'=2,'row'=8,'col'=16] {'aux','row','col'}, use_global_device_ids=true, to_apply=%region_0.1 | all-reduce | flops 4096 | bytes 32768 | tf_op jit(solution)/shard_map/psum | solution.py:77
  576.7 0.6 multiply_bitcast_fusion
  (1 shorter events, 0.0 us)
Async XLA Ops:
  11.1 58.8 %copy-start = (bf16[256,2048]{1,0:T(8,128)(2,1)S(1)}, bf16[256,2048]{1,0:T(8,128)(2,1)}, u32[]{:S(2)}) copy-start(bf16[256,2048]{1,0:T(8,128)(2,1)} %param.5) | copy-start | bytes 3145732
  74.1 270.2 %all-to-all-start.1 = ((bf16[8,256,2048]{2,1,0:T(8,128)(2,1)}), bf16[8,256,2048]{2,1,0:T(8,128)(2,1)}, u32[]{:S(2)}, u32[]{:S(2)}) async-start(bf16[8,256,2048]{2,1,0:T(8,128)(2,1)} %stack.2), calls=%async_computation.1 | async-start | bytes 16777216 | tf_op jit(solution)/shard_map/all_to_all | solution.py:12
  79.1 322.8 %all-gather.2.cloned.1.call-start = ((), (), s32[]{:S(2)}) async-start(), calls=%async_computation.5 | async-start | bytes 9437184 | tf_op jit(solution)/shard_map/all_gather | solution.py:47
  464.2 29.6 %all-to-all-start.4 = ((bf16[32,1,1,16,16,128]{5,3,0,2,1,4:T(8,128)(2,1)}), bf16[32,1,1,16,16,128]{5,3,0,2,1,4:T(8,128)(2,1)}, u32[]{:S(2)}, u32[]{:S(2)}) async-start(bf16[32,1,1,16,16,128]{5,3,0,2,1,4:T(8,128)(2,1)} %copy.21), calls=%async_computation.4 | async-start | bytes 4194304 | tf_op jit(solution)/shard_map/all_to_all | solution.py:60
  468.8 27.9 %collective-permute-start = (bf16[32,256,128]{2,0,1:T(8,128)(2,1)S(1)}, bf16[32,256,128]{2,0,1:T(8,128)(2,1)}, u32[]{:S(2)}, u32[]{:S(2)}) collective-permute-start(bf16[32,256,128]{2,0,1:T(8,128)(2,1)S(1)} %copy_multiply_fusion), channel_id=1, source_target_pairs={{0,128},{128,0},{1,129},{129,1},{2,130},{130,2},{3,131},{131,3},{4... | collective-permute-start | bytes 6291464 | tf_op jit(solution)/shard_map/ppermute | solution.py:23
Sparse Core Ops, SparseCore 0:
  81.8 259.0 all-gather.1
